TPU v7x, 256 devices: a whole 4x4x8 slice. The times are simulated.
256 devices in a mesh: dp: 4 (over y), mp: 64 (over x, z, core).
Axes of the slice: x: 4, y: 4, z: 8, core: 2. Of those that a mesh axis runs over, the one named last changes fastest.
Arguments:
- inputs: bfloat16 [8, 256, 6144], P('dp', None, 'mp'), may hold values from -6 to 6
- cotangent: bfloat16 [8, 256, 6144], P('dp', None, 'mp'), may hold values from -6 to 6
- w_up: bfloat16 [6144, 24576], P('dp', 'mp'), may hold values from -0.078125 to 0.078125
- w_down: bfloat16 [24576, 6144], P('mp', 'dp'), may hold values from -0.0390625 to 0.0390625
- thresholds: float32 [2], replicated, may hold values from 23592.96 to 58982.4
Outputs:
- grad_up: float32 [6144, 24576], P('dp', 'mp')
- grad_down: float32 [24576, 6144], P('mp', 'dp')
- norms: float32 [8, 2], P('dp')
All inputs are finite; a program needn't handle non-finite values.
Results may differ from a plain program's by a relative error of at most 0.0085.
Values may be sent and summed in bfloat16 or wider, within the bound.
A program may use at most 128 MiB of HBM per device.

v0:
```python
import jax
import jax.numpy as jnp
from jax import lax
from jax.sharding import PartitionSpec as P

inv_root_two = 0.7071067811865476
inv_root_two_pi = 0.3989422804014327


def sent_to_all(shard, axis):
    copies = jnp.broadcast_to(shard, (lax.axis_size(axis), *shard.shape))
    return lax.all_to_all(copies, axis, split_axis=0, concat_axis=0, tiled=True)


def taken_together(shard, axis):
    return sent_to_all(shard, axis).sum(axis=0)


def packed_total(arrays, axis):
    line, at, outs = (jnp.concatenate([a.reshape(-1) for a in arrays]), 0, [])
    running = taken_together(line, axis)
    for a in arrays:
        outs.append(running[at : at + a.size].reshape(a.shape))
        at += a.size
    return tuple(outs)


def split_up(shard, dim, count):
    shape = shard.shape
    pieces = shard.reshape(*shape[:dim], count, shape[dim] // count, *shape[dim + 1 :])
    return jnp.moveaxis(pieces, dim, 0)


def sum_at_owner(shard, axis, dim):
    pieces = split_up(shard, dim, lax.axis_size(axis))
    arrived = lax.all_to_all(pieces, axis, split_axis=0, concat_axis=0, tiled=True)
    return arrived.astype(jnp.float32).sum(axis=0)


def normal_cdf(value):
    return 0.5 * (1.0 + lax.erf(value * inv_root_two))


def gram_of(array, images, patches):
    cube = array.reshape(images, patches, -1)
    return jnp.einsum("btd,bsd->bts", cube, cube, preferred_element_type=jnp.float32)


def on_device(inputs, cotangent, w_up, w_down, thresholds):
    images, patches, local_feats = inputs.shape
    count_rows = images * patches
    x_whole = lax.all_gather(inputs, "mp", axis=2, tiled=True).reshape(count_rows, -1)
    hidden_local = w_up.shape[1]
    columns = x_whole
    pre = jnp.dot(
        columns, lax.all_gather(w_up, "dp", axis=0, tiled=True), preferred_element_type=jnp.float32
    )
    act = (pre * normal_cdf(pre)).astype(jnp.bfloat16)
    dy_whole = lax.all_gather(cotangent, "mp", axis=2, tiled=True).reshape(count_rows, -1)
    columns = dy_whole
    dact = lax.dot_general(
        columns,
        lax.all_gather(w_down, "dp", axis=1, tiled=True),
        (((1,), (1,)), ((), ())),
        preferred_element_type=jnp.float32,
    )
    slope = normal_cdf(pre) + pre * jnp.exp(-0.5 * pre * pre) * inv_root_two_pi
    dpre = (dact * slope).astype(jnp.bfloat16)
    gram_dpre = gram_of(dpre, images, patches)
    gram_act = gram_of(act, images, patches)
    part_up = jnp.sum(gram_of(x_whole, images, patches) * gram_dpre, axis=(1, 2))
    part_down = jnp.sum(gram_act * gram_of(dy_whole, images, patches), axis=(1, 2))
    sq_up, sq_down = packed_total((part_up, part_down), "mp")
    norms = jnp.stack([jnp.sqrt(sq_up), jnp.sqrt(sq_down)], axis=1)
    factor = jnp.minimum(1.0, thresholds[None, :] / (norms + 1e-06))
    dpre_clip = (
        (
            factor[:, 0][:, None, None]
            * dpre.reshape(images, patches, hidden_local).astype(jnp.float32)
        )
        .astype(jnp.bfloat16)
        .reshape(count_rows, hidden_local)
    )
    cot_clip = (
        (factor[:, 1][:, None, None] * dy_whole.reshape(images, patches, -1).astype(jnp.float32))
        .astype(jnp.bfloat16)
        .reshape(count_rows, -1)
    )
    columns = x_whole
    grad_up = lax.psum_scatter(
        lax.dot_general(
            columns, dpre_clip, (((0,), (0,)), ((), ())), preferred_element_type=jnp.float32
        ).astype(jnp.bfloat16),
        "dp",
        scatter_dimension=0,
        tiled=True,
    ).astype(jnp.float32)
    down_full = lax.dot_general(
        act, cot_clip, (((0,), (0,)), ((), ())), preferred_element_type=jnp.float32
    )
    grad_down = sum_at_owner(down_full.astype(jnp.bfloat16), "dp", 1)
    return (grad_up, grad_down, norms)


def solution(mesh):
    in_specs = (P("dp", None, "mp"), P("dp", None, "mp"), P("dp", "mp"), P("mp", "dp"), P())
    out_specs = (P("dp", "mp"), P("mp", "dp"), P("dp", None))
    return jax.shard_map(
        on_device, mesh=mesh, in_specs=in_specs, out_specs=out_specs, check_vma=False
    )
```

profile of v0, /device:TPU:1, one launch (start us, length us, event | category | flops | bytes accessed | tf_op | source)
XLA Modules:
  0.0 445.1 jit_solution(11769768210793305239)
XLA Ops:
  7.2 0.0 all-gather.5.cloned.1.call-start
  7.2 0.7 all-gather.5.cloned.1.call-update
  7.9 0.0 all-gather.7.cloned.1.call-start
  7.9 0.7 all-gather.7.cloned.1.call-update
  8.6 0.0 all-gather.11.cloned.1.call-start
  8.7 0.7 all-gather.11.cloned.1.call-update
  9.4 0.0 all-gather.9.cloned.1.call-start
  9.4 0.5 all-gather.9.cloned.1.call-update
  10.0 85.6 %all-gather.5.cloned.1.call-done = bf16[2,256,6144]{1,2,0:T(8,128)(2,1)} async-done(((bf16[2,256,96]{1,2,0:T(8,128)(2,1)}), bf16[2,256,6144]{1,2,0:T(8,128)(2,1)}) %all-gather.5.cloned.1.call-update) | async-done | bytes 6291472 | tf_op jit(solution)/shard_map/all_gather | solution.py:52
  95.5 8.7 %copy.32 = bf16[2,256,6144]{2,1,0:T(8,128)(2,1)} copy(bf16[2,256,6144]{1,2,0:T(8,128)(2,1)} %all-gather.5.cloned.1.call-done) | data formatting | bytes 12582912 | tf_op jit(solution)/shard_map/all_gather | solution.py:52
  104.2 71.4 %all-gather.7.cloned.1.call-done = bf16[2,256,6144]{1,2,0:T(8,128)(2,1)} async-done(((bf16[2,256,96]{1,2,0:T(8,128)(2,1)}), bf16[2,256,6144]{1,2,0:T(8,128)(2,1)}) %all-gather.7.cloned.1.call-update) | async-done | bytes 6291472 | tf_op jit(solution)/shard_map/all_gather | solution.py:59
  175.6 8.7 %copy.31 = bf16[2,256,6144]{2,1,0:T(8,128)(2,1)} copy(bf16[2,256,6144]{1,2,0:T(8,128)(2,1)} %all-gather.7.cloned.1.call-done) | data formatting | bytes 12582912 | tf_op jit(solution)/shard_map/all_gather | solution.py:59
  184.3 44.5 %all-gather.11.cloned.1.call-done = bf16[6144,384]{1,0:T(8,128)(2,1)} async-done(((bf16[1536,384]{1,0:T(8,128)(2,1)}), bf16[6144,384]{1,0:T(8,128)(2,1)}) %all-gather.11.cloned.1.call-update) | async-done | bytes 4718608 | tf_op jit(solution)/shard_map/all_gather | solution.py:56
  228.8 7.0 %multiply_convert_fusion.2 = (bf16[512,384]{1,0:T(8,128)(2,1)S(1)}, f32[512,384]{1,0:T(8,128)S(1)}) fusion(bf16[512,6144]{1,0:T(8,128)(2,1)} %bitcast.47, bf16[6144,384]{1,0:T(8,128)(2,1)} %all-gather.11.cloned.1.call-done), kind=kOutput, calls=%fused_computation.18 | convolution fusion | flops 2416902144 | bytes 12189696 | tf_op jit(solution)/shard_map/dot_general | solution.py:55
  235.7 50.3 %all-gather.9.cloned.1.call-done = bf16[384,6144]{1,0:T(8,128)(2,1)} async-done(((bf16[384,1536]{1,0:T(8,128)(2,1)}), bf16[384,6144]{1,0:T(8,128)(2,1)}) %all-gather.9.cloned.1.call-update) | async-done | bytes 4718608 | tf_op jit(solution)/shard_map/all_gather | solution.py:63
  286.0 7.7 %fusion.1 = bf16[512,384]{1,0:T(8,128)(2,1)S(1)} fusion(bf16[512,6144]{1,0:T(8,128)(2,1)} %bitcast.46, bf16[384,6144]{1,0:T(8,128)(2,1)} %all-gather.9.cloned.1.call-done, f32[512,384]{1,0:T(8,128)S(1)} %get-tuple-element.25), kind=kOutput, calls=%fused_computation.7 | convolution fusion | flops 2417885184 | bytes 12189696 | tf_op jit(solution)/shard_map/dot_general | solution.py:61
  293.7 0.3 fusion.9
  294.0 0.0 slice-start
  294.0 0.3 fusion.10
  294.4 0.0 slice-start.1
  294.4 7.4 %fusion.2 = f32[2]{0:T(128)S(1)} fusion(f32[2,256,256]{2,1,0:T(8,128)S(1)} %fusion.9, bf16[2,256,6144]{1,2,0:T(8,128)(2,1)} %all-gather.5.cloned.1.call-done), kind=kOutput, calls=%fused_computation.11 | convolution fusion | flops 1610874880 | bytes 6815752 | tf_op jit(solution)/shard_map/btd,bsd->bts/dot_general | solution.py:46
  301.8 0.0 slice-done
  301.8 0.0 slice-done.1
  301.8 0.0 copy-start
  301.8 2.7 fusion.3
  304.5 0.1 pad_maximum_fusion.1
  304.6 0.6 broadcast_in_dim.4
  305.2 10.8 %all-to-all-start = ((f32[64,1,4]{2,1,0:T(1,128)}), f32[64,1,4]{2,1,0:T(1,128)S(1)}, u32[]{:S(2)}, u32[]{:S(2)}) async-start(f32[64,1,4]{2,1,0:T(1,128)} %broadcast_in_dim.4), calls=%async_computation | async-start | bytes 65536 | tf_op jit(solution)/shard_map/all_to_all | solution.py:12
  316.1 0.2 reduce-scatter.2.cloned.1.call-start
  316.3 0.2 copy.34
  316.5 8.8 %all-to-all-done = f32[64,1,4]{2,1,0:T(1,128)S(1)} async-done(((f32[64,1,4]{2,1,0:T(1,128)}), f32[64,1,4]{2,1,0:T(1,128)S(1)}, u32[]{:S(2)}, u32[]{:S(2)}) %all-to-all-start) | async-done | bytes 1056 | tf_op jit(solution)/shard_map/all_to_all | solution.py:12
  325.3 0.1 reduce_sum.38
  325.4 0.1 sqrt_bitcast_fusion.1
  325.5 0.0 copy-done
  325.5 0.1 pad_maximum_fusion
  325.5 8.6 %fusion = bf16[6144,384]{0,1:T(8,128)(2,1)} fusion(bf16[2,256,6144]{1,2,0:T(8,128)(2,1)} %all-gather.5.cloned.1.call-done, bf16[2,256,384]{1,2,0:T(8,128)(2,1)S(1)} %copy.34, f32[2]{0:T(128)S(1)} %get-tuple-element.21), kind=kOutput, calls=%fused_computation.4 | convolution fusion | flops 2418868224 | bytes 11403272 | tf_op jit(solution)/shard_map/dot_general | solution.py:91
  334.2 0.0 reduce-scatter.2.cloned.1.call-update
  334.2 7.5 %multiply_convert_fusion = bf16[2,256,6144]{1,2,0:T(8,128)(2,1)} fusion(bf16[2,256,6144]{1,2,0:T(8,128)(2,1)} %all-gather.7.cloned.1.call-done, f32[2]{0:T(128)S(1)} %get-tuple-element.20), kind=kLoop, calls=%fused_computation | loop fusion | flops 9437184 | bytes 12582920 | tf_op jit(solution)/shard_map/convert_element_type | solution.py:86
  341.7 8.7 %copy.35 = bf16[2,256,6144]{2,1,0:T(8,128)(2,1)} copy(bf16[2,256,6144]{1,2,0:T(8,128)(2,1)} %multiply_convert_fusion) | data formatting | bytes 12582912 | tf_op jit(solution)/shard_map/convert_element_type | solution.py:86
  350.4 5.4 %convolution_convert_fusion = bf16[384,6144]{1,0:T(8,128)(2,1)S(1)} fusion(bf16[512,384]{1,0:T(8,128)(2,1)S(1)} %get-tuple-element.24, bf16[512,6144]{1,0:T(8,128)(2,1)} %bitcast.43), kind=kOutput, calls=%fused_computation.3 | convolution fusion | flops 2418278400 | bytes 11403264 | tf_op jit(solution)/shard_map/dot_general | solution.py:98
  355.8 2.6 copy.44
  358.4 4.9 %all-to-all-start.1 = ((bf16[4,384,1536]{2,1,0:T(8,128)(2,1)}), bf16[4,384,1536]{2,1,0:T(8,128)(2,1)}, u32[]{:S(2)}, u32[]{:S(2)}) async-start(bf16[4,384,1536]{2,1,0:T(8,128)(2,1)} %bitcast.44), calls=%async_computation.2 | async-start | bytes 9437184 | tf_op jit(solution)/shard_map/all_to_all | solution.py:36
  363.3 0.6 copy.38
  364.0 67.2 %all-to-all-done.1 = bf16[4,384,1536]{2,1,0:T(8,128)(2,1)} async-done(((bf16[4,384,1536]{2,1,0:T(8,128)(2,1)}), bf16[4,384,1536]{2,1,0:T(8,128)(2,1)}, u32[]{:S(2)}, u32[]{:S(2)}) %all-to-all-start.1) | async-done | bytes 4718624 | tf_op jit(solution)/shard_map/all_to_all | solution.py:36
  431.2 4.7 %convert_reduce_fusion = f32[384,1536]{1,0:T(8,128)} fusion(bf16[4,384,1536]{2,1,0:T(8,128)(2,1)} %all-to-all-done.1), kind=kLoop, calls=%fused_computation.2 | loop fusion | flops 4128768 | bytes 7077888 | tf_op jit(solution)/shard_map/reduce_sum | solution.py:37
  435.9 0.0 reduce-scatter.2.cloned.1.call-done
  435.9 2.7 copy.37
  (2 shorter events, 0.0 us)
Async XLA Ops:
  7.2 88.4 %all-gather.5.cloned.1.call-start = ((), (), s32[]{:S(2)}) async-start(), calls=%async_computation.3 | async-start | bytes 6389760 | tf_op jit(solution)/shard_map/all_gather | solution.py:52
  7.9 167.7 %all-gather.7.cloned.1.call-start = ((), (), s32[]{:S(2)}) async-start(), calls=%async_computation.4 | async-start | bytes 6389760 | tf_op jit(solution)/shard_map/all_gather | solution.py:59
  8.6 220.1 %all-gather.11.cloned.1.call-start = ((), (), s32[]{:S(2)}) async-start(), calls=%async_computation.6 | async-start | bytes 5898240 | tf_op jit(solution)/shard_map/all_gather | solution.py:56
  9.4 276.6 %all-gather.9.cloned.1.call-start = ((), (), s32[]{:S(2)}) async-start(), calls=%async_computation.5 | async-start | bytes 5898240 | tf_op jit(solution)/shard_map/all_gather | solution.py:63
  294.0 7.8 %slice-start = ((s8[6291456]{0:T(1024)(128)(4,1)}), s8[4194304]{0:T(1024)(128)(4,1)S(1)}, s32[]{:S(2)}) async-start(s8[6291456]{0:T(1024)(128)(4,1)} %bitcast.41), calls=%async_computation.8 | async-start | bytes 8388608
  294.4 7.4 %slice-start.1 = ((s8[6291456]{0:T(1024)(128)(4,1)}), s8[2097152]{0:T(1024)(128)(4,1)S(1)}, s32[]{:S(2)}) async-start(s8[6291456]{0:T(1024)(128)(4,1)} %bitcast.41), calls=%async_computation.9 | async-start | bytes 4194304
  301.8 23.7 %copy-start = (f32[2]{0:T(128)S(1)}, f32[2]{0:T(128)}, u32[]{:S(2)}) copy-start(f32[2]{0:T(128)} %param.9) | copy-start | bytes 28
  305.2 20.1 %all-to-all-start = ((f32[64,1,4]{2,1,0:T(1,128)}), f32[64,1,4]{2,1,0:T(1,128)S(1)}, u32[]{:S(2)}, u32[]{:S(2)}) async-start(f32[64,1,4]{2,1,0:T(1,128)} %broadcast_in_dim.4), calls=%async_computation | async-start | bytes 65536 | tf_op jit(solution)/shard_map/all_to_all | solution.py:12
  316.1 119.8 %reduce-scatter.2.cloned.1.call-start = ((), (), s32[]{:S(2)}) async-start(), calls=%async_computation.7 | async-start | bytes 5898240 | tf_op jit(solution)/shard_map/reduce_scatter | solution.py:90
  358.4 72.8 %all-to-all-start.1 = ((bf16[4,384,1536]{2,1,0:T(8,128)(2,1)}), bf16[4,384,1536]{2,1,0:T(8,128)(2,1)}, u32[]{:S(2)}, u32[]{:S(2)}) async-start(bf16[4,384,1536]{2,1,0:T(8,128)(2,1)} %bitcast.44), calls=%async_computation.2 | async-start | bytes 9437184 | tf_op jit(solution)/shard_map/all_to_all | solution.py:36
Sparse Core Ops, SparseCore 0:
  10.8 84.6 all-gather.4
  98.3 77.2 all-gather.6
  177.4 51.2 all-gather.10
  230.4 55.5 all-gather.8
  334.3 59.8 reduce-scatter.1
where the time goes:
time: 446 us; the launch traced here: 445 us
  waiting for transfers between devices  330 us (74%)
  matrix products  39.5 us (9%)
  local copies, waits for them, and re-layouts  32.9 us (7%)
  starting transfers between devices  16.1 us (4%)
  between operations  13.9 us (3%)
  other arithmetic  12.4 us (3%)
    all_gather x1, waiting for transfers between devices, on_device(): lax.all_gather(inputs, 'mp', axis=2, tiled=True).reshape(count_rows, -1)  85.6 us
    all_gather x1, waiting for transfers between devices, on_device(): lax.all_gather(cotangent, 'mp', axis=2, tiled=True).reshape(count_rows, -1)  71.4 us
    all_to_all x1, waiting for transfers between devices, sum_at_owner(): lax.all_to_all(pieces, axis, split_axis=0, concat_axis=0, tiled=True)  67.2 us
    all_gather x1, waiting for transfers between devices, on_device(): lax.all_gather(w_down, 'dp', axis=1, tiled=True)  50.3 us
    all_gather x1, waiting for transfers between devices, on_device(): lax.all_gather(w_up, 'dp', axis=0, tiled=True)  44.5 us
    all_to_all x1, starting transfers between devices, sent_to_all(): return lax.all_to_all(copies, axis, split_axis=0, concat_axis=0, tiled=True)  10.8 us
    dot_general x4, matrix products, gram_of(): jnp.einsum('btd,bsd->bts', cube, cube, preferred_element_type=jnp.float32)  10.8 us
  transfers between devices with their start and end apart: 7, of which 6 were waited for; matrix products, arithmetic and copies ran while one was open for 12% of the time, Pallas kernels for 0%

commit v1 on v0

--- a/solution.py
+++ b/solution.py
@@ -56,7 +56,7 @@
         columns, lax.all_gather(w_up, "dp", axis=0, tiled=True), preferred_element_type=jnp.float32
     )
     act = (pre * normal_cdf(pre)).astype(jnp.bfloat16)
-    dy_whole = lax.all_gather(cotangent, "mp", axis=2, tiled=True).reshape(count_rows, -1)
+    dy_whole = jnp.concatenate(lax.all_gather(cotangent, "mp"), axis=2).reshape(count_rows, -1)
     columns = dy_whole
     dact = lax.dot_general(
         columns,

time: 446 us -> 446 us (level)
  other arithmetic: 12.4 us -> 4.91 us
  waiting for transfers between devices: 330 us -> 336 us
    all_gather x1, waiting for transfers between devices: 85.6 us -> 61.1 us  [on_device(): lax.all_gather(inputs, 'mp', axis=2, tiled=True).reshape(count_rows, -1)]
    all_to_all x1, waiting for transfers between devices: 67.2 us -> 83.3 us  [sum_at_owner(): lax.all_to_all(pieces, axis, split_axis=0, concat_axis=0, tiled=True)]
    reshape x0 -> x2, local copies, waits for them, and re-layouts: none -> 15.1 us  [on_device(): jnp.concatenate(lax.all_gather(cotangent, 'mp'), axis=2)]
    all_gather x1, waiting for transfers between devices: 71.4 us -> 85.5 us  [on_device(): lax.all_gather(cotangent, 'mp')]
    all_gather x1 -> x0, local copies, waits for them, and re-layouts: 8.68 us -> none  [on_device(): lax.all_gather(cotangent, 'mp', axis=2, tiled=True).reshape(count_rows, -1)]
    convert_element_type x1 -> x0, local copies, waits for them, and re-layouts: 8.68 us -> none  [on_device(): cot_clip = (factor[:, 1][:, None, None] * dy_whole.reshape(images, patche...]
    convert_element_type x1 -> x0, other arithmetic: 7.52 us -> none  [on_device(): cot_clip = (factor[:, 1][:, None, None] * dy_whole.reshape(images, patche...]
  transfers between devices with their start and end apart: 7 -> 7, of which waited for: 6 -> 6; matrix products, arithmetic and copies ran while one was open for 12% -> 11% of each run, Pallas kernels for 0% -> 0%
where the time goes in v1:
time: 446 us; the launch traced here: 445 us
  waiting for transfers between devices  336 us (75%)
  matrix products  39.9 us (9%)
  local copies, waits for them, and re-layouts  34.4 us (8%)
  starting transfers between devices  16 us (4%)
  between operations  13.9 us (3%)
  other arithmetic  4.91 us (1%)
    all_gather x1, waiting for transfers between devices, on_device(): lax.all_gather(cotangent, 'mp')  85.5 us
    all_to_all x1, waiting for transfers between devices, sum_at_owner(): lax.all_to_all(pieces, axis, split_axis=0, concat_axis=0, tiled=True)  83.3 us
    all_gather x1, waiting for transfers between devices, on_device(): lax.all_gather(inputs, 'mp', axis=2, tiled=True).reshape(count_rows, -1)  61.1 us
    all_gather x1, waiting for transfers between devices, on_device(): lax.all_gather(w_down, 'dp', axis=1, tiled=True)  50.1 us
    all_gather x1, waiting for transfers between devices, on_device(): lax.all_gather(w_up, 'dp', axis=0, tiled=True)  44.5 us
    reshape x2, local copies, waits for them, and re-layouts, on_device(): jnp.concatenate(lax.all_gather(cotangent, 'mp'), axis=2)  15.1 us
    all_to_all x1, starting transfers between devices, sent_to_all(): return lax.all_to_all(copies, axis, split_axis=0, concat_axis=0, tiled=True)  10.8 us
    dot_general x4, matrix products, gram_of(): jnp.einsum('btd,bsd->bts', cube, cube, preferred_element_type=jnp.float32)  10.7 us
  transfers between devices with their start and end apart: 7, of which 6 were waited for; matrix products, arithmetic and copies ran while one was open for 11% of the time, Pallas kernels for 0%

profile of v1, /device:TPU:1, one launch (start us, length us, event | category | flops | bytes accessed | tf_op | source)
XLA Modules:
  0.0 445.3 jit_solution(8081282076292831385)
XLA Ops:
  7.2 0.0 all-gather.12.cloned.1.call-start
  7.2 0.7 all-gather.12.cloned.1.call-update
  7.9 0.0 all-gather.6.cloned.1.call-start
  7.9 0.7 all-gather.6.cloned.1.call-update
  8.6 0.0 all-gather.10.cloned.1.call-start
  8.7 0.7 all-gather.10.cloned.1.call-update
  9.4 0.0 all-gather.8.cloned.1.call-start
  9.4 0.5 all-gather.8.cloned.1.call-update
  10.0 85.5 %all-gather.12.cloned.1.call-done = bf16[128,256,96]{1,2,0:T(8,128)(2,1)} async-done(((bf16[2,256,96]{1,2,0:T(8,128)(2,1)}), bf16[128,256,96]{1,2,0:T(8,128)(2,1)}) %all-gather.12.cloned.1.call-update) | async-done | bytes 6291472 | tf_op jit(solution)/shard_map/all_gather | solution.py:59
  95.4 0.0 copy-start
  95.5 12.1 %copy.45 = bf16[2,256,64,96]{1,0,3,2:T(2,128)(2,1)S(1)} copy(bf16[2,256,64,96]{1,3,0,2:T(8,128)(2,1)} %bitcast.53) | data formatting | bytes 12582912 | tf_op jit(solution)/shard_map/reshape | solution.py:59
  107.5 0.0 copy-done
  107.6 3.0 copy.47
  110.6 3.8 copy.61
  114.4 61.1 %all-gather.6.cloned.1.call-done = bf16[2,256,6144]{1,2,0:T(8,128)(2,1)} async-done(((bf16[2,256,96]{1,2,0:T(8,128)(2,1)}), bf16[2,256,6144]{1,2,0:T(8,128)(2,1)}) %all-gather.6.cloned.1.call-update) | async-done | bytes 6291472 | tf_op jit(solution)/shard_map/all_gather | solution.py:52
  175.5 8.6 %copy.46 = bf16[2,256,6144]{2,1,0:T(8,128)(2,1)} copy(bf16[2,256,6144]{1,2,0:T(8,128)(2,1)} %all-gather.6.cloned.1.call-done) | data formatting | bytes 12582912 | tf_op jit(solution)/shard_map/all_gather | solution.py:52
  184.1 44.5 %all-gather.10.cloned.1.call-done = bf16[6144,384]{1,0:T(8,128)(2,1)} async-done(((bf16[1536,384]{1,0:T(8,128)(2,1)}), bf16[6144,384]{1,0:T(8,128)(2,1)}) %all-gather.10.cloned.1.call-update) | async-done | bytes 4718608 | tf_op jit(solution)/shard_map/all_gather | solution.py:56
  228.6 7.1 %multiply_convert_fusion.3 = (bf16[512,384]{1,0:T(8,128)(2,1)S(1)}, f32[512,384]{1,0:T(8,128)S(1)}) fusion(bf16[512,6144]{1,0:T(8,128)(2,1)} %bitcast.59, bf16[6144,384]{1,0:T(8,128)(2,1)} %all-gather.10.cloned.1.call-done), kind=kOutput, calls=%fused_computation.19 | convolution fusion | flops 2416902144 | bytes 12189696 | tf_op jit(solution)/shard_map/dot_general | solution.py:55
  235.8 50.1 %all-gather.8.cloned.1.call-done = bf16[384,6144]{1,0:T(8,128)(2,1)} async-done(((bf16[384,1536]{1,0:T(8,128)(2,1)}), bf16[384,6144]{1,0:T(8,128)(2,1)}) %all-gather.8.cloned.1.call-update) | async-done | bytes 4718608 | tf_op jit(solution)/shard_map/all_gather | solution.py:63
  285.9 7.7 %fusion.2 = bf16[512,384]{1,0:T(8,128)(2,1)S(1)} fusion(bf16[512,6144]{0,1:T(8,128)(2,1)} %bitcast.57, bf16[384,6144]{1,0:T(8,128)(2,1)} %all-gather.8.cloned.1.call-done, f32[512,384]{1,0:T(8,128)S(1)} %get-tuple-element.28), kind=kOutput, calls=%fused_computation.8 | convolution fusion | flops 2417885184 | bytes 12189696 | tf_op jit(solution)/shard_map/dot_general | solution.py:61
  293.6 0.3 fusion.10
  293.9 0.0 slice-start
  293.9 0.3 fusion.11
  294.3 0.0 slice-start.1
  294.3 7.4 %fusion.4 = f32[2]{0:T(128)S(1)} fusion(f32[2,256,256]{2,1,0:T(8,128)S(1)} %fusion.11, bf16[2,256,6144]{1,2,0:T(8,128)(2,1)} %bitcast.52), kind=kOutput, calls=%fused_computation.13 | convolution fusion | flops 1610874880 | bytes 6815752 | tf_op jit(solution)/shard_map/btd,bsd->bts/dot_general | solution.py:46
  301.7 0.0 slice-done
  301.7 0.0 slice-done.1
  301.7 0.0 copy-start.1
  301.7 2.7 fusion.3
  304.4 0.1 pad_maximum_fusion.1
  304.5 0.6 broadcast_in_dim.4
  305.1 10.8 %all-to-all-start = ((f32[64,1,4]{2,1,0:T(1,128)}), f32[64,1,4]{2,1,0:T(1,128)S(1)}, u32[]{:S(2)}, u32[]{:S(2)}) async-start(f32[64,1,4]{2,1,0:T(1,128)} %broadcast_in_dim.4), calls=%async_computation | async-start | bytes 65536 | tf_op jit(solution)/shard_map/all_to_all | solution.py:12
  316.0 0.0 reduce-scatter.2.cloned.1.call-start
  316.0 0.2 copy.51
  316.2 9.0 %all-to-all-done = f32[64,1,4]{2,1,0:T(1,128)S(1)} async-done(((f32[64,1,4]{2,1,0:T(1,128)}), f32[64,1,4]{2,1,0:T(1,128)S(1)}, u32[]{:S(2)}, u32[]{:S(2)}) %all-to-all-start) | async-done | bytes 1056 | tf_op jit(solution)/shard_map/all_to_all | solution.py:12
  325.2 0.1 reduce_sum.38
  325.3 0.1 sqrt_bitcast_fusion.1
  325.4 0.0 copy-done.1
  325.4 0.1 pad_maximum_fusion
  325.4 8.8 %fusion = bf16[6144,384]{0,1:T(8,128)(2,1)} fusion(bf16[2,256,6144]{1,2,0:T(8,128)(2,1)} %all-gather.6.cloned.1.call-done, bf16[2,256,384]{1,2,0:T(8,128)(2,1)S(1)} %copy.51, f32[2]{0:T(128)S(1)} %get-tuple-element.24), kind=kOutput, calls=%fused_computation.4 | convolution fusion | flops 2418868224 | bytes 11403272 | tf_op jit(solution)/shard_map/dot_general | solution.py:91
  334.3 0.0 reduce-scatter.2.cloned.1.call-update
  334.3 0.1 broadcast_bitcast_fusion
  334.4 5.5 %convolution_convert_fusion = bf16[384,6144]{1,0:T(8,128)(2,1)S(1)} fusion(bf16[512,384]{1,0:T(8,128)(2,1)S(1)} %get-tuple-element.27, bf16[512,6144]{0,1:T(8,128)(2,1)} %bitcast.58, f32[512]{0:T(512)S(1)} %bitcast.64), kind=kOutput, calls=%fused_computation.3 | convolution fusion | flops 2427715584 | bytes 11405312 | tf_op jit(solution)/shard_map/dot_general | solution.py:98
  339.8 2.5 copy.64
  342.4 5.0 %all-to-all-start.1 = ((bf16[4,384,1536]{2,1,0:T(8,128)(2,1)}), bf16[4,384,1536]{2,1,0:T(8,128)(2,1)}, u32[]{:S(2)}, u32[]{:S(2)}) async-start(bf16[4,384,1536]{2,1,0:T(8,128)(2,1)} %bitcast.56), calls=%async_computation.2 | async-start | bytes 9437184 | tf_op jit(solution)/shard_map/all_to_all | solution.py:36
  347.4 0.6 copy.54
  348.0 83.3 %all-to-all-done.1 = bf16[4,384,1536]{2,1,0:T(8,128)(2,1)} async-done(((bf16[4,384,1536]{2,1,0:T(8,128)(2,1)}), bf16[4,384,1536]{2,1,0:T(8,128)(2,1)}, u32[]{:S(2)}, u32[]{:S(2)}) %all-to-all-start.1) | async-done | bytes 4718624 | tf_op jit(solution)/shard_map/all_to_all | solution.py:36
  431.3 4.7 %convert_reduce_fusion = f32[384,1536]{1,0:T(8,128)} fusion(bf16[4,384,1536]{2,1,0:T(8,128)(2,1)} %all-to-all-done.1), kind=kLoop, calls=%fused_computation.2 | loop fusion | flops 4128768 | bytes 7077888 | tf_op jit(solution)/shard_map/reduce_sum | solution.py:37
  436.0 0.0 reduce-scatter.2.cloned.1.call-done
  436.0 2.7 copy.53
  (3 shorter events, 0.0 us)
Async XLA Ops:
  7.2 88.3 %all-gather.12.cloned.1.call-start = ((), (), s32[]{:S(2)}) async-start(), calls=%async_computation.7 | async-start | bytes 6389760 | tf_op jit(solution)/shard_map/all_gather | solution.py:59
  7.9 167.6 %all-gather.6.cloned.1.call-start = ((), (), s32[]{:S(2)}) async-start(), calls=%async_computation.3 | async-start | bytes 6389760 | tf_op jit(solution)/shard_map/all_gather | solution.py:52
  8.6 220.0 %all-gather.10.cloned.1.call-start = ((), (), s32[]{:S(2)}) async-start(), calls=%async_computation.5 | async-start | bytes 5898240 | tf_op jit(solution)/shard_map/all_gather | solution.py:56
  9.4 276.5 %all-gather.8.cloned.1.call-start = ((), (), s32[]{:S(2)}) async-start(), calls=%async_computation.4 | async-start | bytes 5898240 | tf_op jit(solution)/shard_map/all_gather | solution.py:63
  95.4 12.1 %copy-start = (bf16[128,256,96]{1,2,0:T(8,128)(2,1)S(1)}, bf16[128,256,96]{1,2,0:T(8,128)(2,1)}, u32[]{:S(2)}) copy-start(bf16[128,256,96]{1,2,0:T(8,128)(2,1)} %all-gather.12.cloned.1.call-done) | copy-start | bytes 18874372
  293.9 7.8 %slice-start = ((s8[6291456]{0:T(1024)(128)(4,1)}), s8[4194304]{0:T(1024)(128)(4,1)S(1)}, s32[]{:S(2)}) async-start(s8[6291456]{0:T(1024)(128)(4,1)} %bitcast.50), calls=%async_computation.8 | async-start | bytes 8388608
  294.3 7.4 %slice-start.1 = ((s8[6291456]{0:T(1024)(128)(4,1)}), s8[2097152]{0:T(1024)(128)(4,1)S(1)}, s32[]{:S(2)}) async-start(s8[6291456]{0:T(1024)(128)(4,1)} %bitcast.50), calls=%async_computation.9 | async-start | bytes 4194304
  301.7 23.7 %copy-start.1 = (f32[2]{0:T(128)S(1)}, f32[2]{0:T(128)}, u32[]{:S(2)}) copy-start(f32[2]{0:T(128)} %param.9) | copy-start | bytes 28
  305.1 20.1 %all-to-all-start = ((f32[64,1,4]{2,1,0:T(1,128)}), f32[64,1,4]{2,1,0:T(1,128)S(1)}, u32[]{:S(2)}, u32[]{:S(2)}) async-start(f32[64,1,4]{2,1,0:T(1,128)} %broadcast_in_dim.4), calls=%async_computation | async-start | bytes 65536 | tf_op jit(solution)/shard_map/all_to_all | solution.py:12
  316.0 120.1 %reduce-scatter.2.cloned.1.call-start = ((), (), s32[]{:S(2)}) async-start(), calls=%async_computation.6 | async-start | bytes 5898240 | tf_op jit(solution)/shard_map/reduce_scatter | solution.py:90
  342.4 88.9 %all-to-all-start.1 = ((bf16[4,384,1536]{2,1,0:T(8,128)(2,1)}), bf16[4,384,1536]{2,1,0:T(8,128)(2,1)}, u32[]{:S(2)}, u32[]{:S(2)}) async-start(bf16[4,384,1536]{2,1,0:T(8,128)(2,1)} %bitcast.56), calls=%async_computation.2 | async-start | bytes 9437184 | tf_op jit(solution)/shard_map/all_to_all | solution.py:36
Sparse Core Ops, SparseCore 0:
  10.7 84.6 all-gather.11
  98.3 77.1 all-gather.5
  177.3 51.2 all-gather.9
  230.3 55.5 all-gather.7
  334.4 75.6 reduce-scatter.1
